TPU v7x, 32 devices: a whole 2x2x4 slice. The times are simulated.
32 devices in a mesh: dp: 8 (over y, x, core), tensor: 4 (over z).
Axes of the slice: x: 2, y: 2, z: 4, core: 2. Of those that a mesh axis runs over, the one named last changes fastest.
Arguments:
- x_in: bfloat16 [16384, 768], P(('dp', 'tensor')), may hold values from -6 to 6
- bucket: int32 [32], P(('dp', 'tensor')), may hold values from 0 to 1
- lengths: int32 [32, 4], P(('dp', 'tensor')), may hold values from 32 to 128, as said below
- qkv_weight: bfloat16 [2, 768, 2304], replicated, may hold values from -0.21875 to 0.21875
- out_weight: bfloat16 [2, 768, 768], replicated, may hold values from -0.875 to 0.875
- norm_gain1: float32 [2, 768], replicated, may hold values from 0.5 to 1.5
- norm_bias1: float32 [2, 768], replicated, may hold values from -1.8 to 1.8
- up_weight: bfloat16 [2, 768, 2, 3072], P(None, None, None, 'tensor'), may hold values from -0.21875 to 0.21875
- down_weight: bfloat16 [2, 3072, 768], P(None, 'tensor'), may hold values from -0.109375 to 0.109375
- norm_gain2: float32 [2, 768], replicated, may hold values from 0.5 to 1.5
- norm_bias2: float32 [2, 768], replicated, may hold values from -1.8 to 1.8
- cotangent: bfloat16 [16384, 768], P(('dp', 'tensor')), may hold values from -6 to 6
Outputs:
- activations: bfloat16 [2, 16384, 768], P(None, ('dp', 'tensor'))
- input_grad: float32 [16384, 768], P(('dp', 'tensor'))
- qkv_grad: float32 [2, 768, 2304], replicated
- out_grad: float32 [2, 768, 768], replicated
- gain1_grad: float32 [2, 768], replicated
- bias1_grad: float32 [2, 768], replicated
- up_grad: float32 [2, 768, 2, 3072], P(None, 'dp', None, 'tensor')
- down_grad: float32 [2, 3072, 768], P(None, 'tensor', 'dp')
- gain2_grad: float32 [2, 768], replicated
- bias2_grad: float32 [2, 768], replicated
Inputs may be any that keep to these rules, and one draw needn't show every extreme that they name: Every entry is a length of a short sequence; each row of lengths has an entry equal to 128. A block of bucket 1 holds one sequence whose length is the sum of its row of lengths.
All inputs are finite; a program needn't handle non-finite values.
Results may differ from a plain program's by a relative error of at most 0.033.
Values may be sent and summed in bfloat16 or wider, within the bound.
No kernel may reach another device: no remote copies, remote signals or barrier semaphores. Data moves between devices by JAX's collectives and lax.ppermute only.
A program may use at most 256 MiB of HBM per device.

v0:
```python
import jax
import jax.numpy as jnp
from jax import lax
from jax.sharding import PartitionSpec as P

HEADS = 12
HEAD_DIM = 64
SHORT = 128
LAYERS = 2
eps_norm = 1e-05
gelu_coef = 0.7978845608028654
masked_score = -1e30


def segments(bucket_one, lens, rows_dev, short_len):
    rows = jnp.arange(rows_dev, dtype=jnp.int32)
    slot = rows // short_len
    offset = rows - slot * short_len
    slots_all = jnp.arange(lens.shape[0], dtype=jnp.int32)
    slot_len = jnp.sum(jnp.where(slot[:, None] == slots_all[None, :], lens[None, :], 0), axis=1)
    total = jnp.sum(lens)
    is_long = bucket_one == 1
    real = jnp.where(is_long, rows < total, offset < slot_len)
    group = jnp.where(is_long, 0, slot)
    return jnp.where(real, group, lens.shape[0] + rows)


def alibi(rows_dev, heads):
    slopes = jnp.exp2(-8.0 * (jnp.arange(heads, dtype=jnp.float32) + 1.0) / heads)
    place = jnp.arange(rows_dev, dtype=jnp.float32)
    dist = jnp.abs(place[:, None] - place[None, :])
    return slopes[:, None, None] * dist[None, :, :]


def layer_norm(value, gain, bias):
    mean = jnp.mean(value, axis=-1, keepdims=True)
    centered = value - mean
    var = jnp.mean(centered * centered, axis=-1, keepdims=True)
    return centered * lax.rsqrt(var + eps_norm) * gain + bias


def geglu(joined):
    half = joined.shape[1] // 2
    gate = joined[:, :half]
    value = joined[:, half:]
    return 0.5 * gate * (1.0 + jnp.tanh(gelu_coef * (gate + 0.044715 * gate * gate * gate))) * value


def split_heads(qkv_low, width):
    rows = qkv_low.shape[0]
    query = qkv_low[:, :width].reshape(rows, HEADS, HEAD_DIM)
    keys = qkv_low[:, width : 2 * width].reshape(rows, HEADS, HEAD_DIM)
    values = qkv_low[:, 2 * width :].reshape(rows, HEADS, HEAD_DIM)
    return (query, keys, values)


def scores_of(query, keys, same, decay):
    raw = (
        jnp.einsum("qhe,khe->hqk", query, keys, preferred_element_type=jnp.float32)
        * HEAD_DIM ** (-0.5)
        - decay
    )
    return jnp.where(same[None, :, :], raw, masked_score)


def forward_layer(x_low, wqkv, wo, g1, b1, wup, wdown, g2, b2, same, decay):
    rows = x_low.shape[0]
    width = x_low.shape[1]
    qkv_low = jnp.dot(x_low, wqkv, preferred_element_type=jnp.float32).astype(jnp.bfloat16)
    query, keys, values = split_heads(qkv_low, width)
    scores = scores_of(query, keys, same, decay)
    top = jnp.max(scores, axis=-1, keepdims=True)
    log_total = top + jnp.log(jnp.sum(jnp.exp(scores - top), axis=-1, keepdims=True))
    probs_low = jnp.exp(scores - log_total).astype(jnp.bfloat16)
    ctx_low = (
        jnp.einsum("hqk,khe->qhe", probs_low, values, preferred_element_type=jnp.float32)
        .reshape(rows, width)
        .astype(jnp.bfloat16)
    )
    attn = jnp.dot(ctx_low, wo, preferred_element_type=jnp.float32)
    pre_first = x_low.astype(jnp.float32) + attn
    normed = layer_norm(pre_first, g1, b1)
    normed_low = normed.astype(jnp.bfloat16)
    gathered = lax.all_gather(normed_low, "tensor", axis=0, tiled=True)
    joined = jnp.dot(gathered, wup.reshape(width, -1), preferred_element_type=jnp.float32)
    act_low = geglu(joined).astype(jnp.bfloat16)
    mixed = lax.psum_scatter(
        jnp.dot(act_low, wdown, preferred_element_type=jnp.float32).astype(jnp.bfloat16),
        "tensor",
        scatter_dimension=0,
        tiled=True,
    ).astype(jnp.float32)
    pre_second = normed + mixed
    out_low = layer_norm(pre_second, g2, b2).astype(jnp.bfloat16)
    keep = (
        x_low,
        qkv_low,
        log_total,
        ctx_low,
        pre_first,
        normed_low,
        pre_second,
        gathered,
        joined,
        act_low,
    )
    return (out_low, keep)


def backward_layer(grad_out, keep, wqkv, wo, g1, b1, wup, wdown, g2, b2, same, decay):
    (
        x_low,
        qkv_low,
        log_total,
        ctx_low,
        pre_first,
        normed_low,
        pre_second,
        gathered,
        joined,
        act_low,
    ) = keep
    rows = x_low.shape[0]
    width = x_low.shape[1]
    up_flat = wup.reshape(width, -1)
    second_pull = jax.vjp(layer_norm, pre_second, g2, b2)[1]
    d_pre2, d_gain2, d_bias2 = second_pull(grad_out)
    grad_rows = lax.all_gather(d_pre2.astype(jnp.bfloat16), "tensor", axis=0, tiled=True)
    d_act = jnp.dot(grad_rows, wdown.T, preferred_element_type=jnp.float32)
    d_down = jnp.dot(act_low.T, grad_rows, preferred_element_type=jnp.float32)
    geglu_pull = jax.vjp(geglu, joined)[1]
    d_joined = geglu_pull(d_act)[0].astype(jnp.bfloat16)
    d_up = jnp.dot(gathered.T, d_joined, preferred_element_type=jnp.float32).reshape(wup.shape)
    d_normed = d_pre2 + lax.psum_scatter(
        jnp.dot(d_joined, up_flat.T, preferred_element_type=jnp.float32).astype(jnp.bfloat16),
        "tensor",
        scatter_dimension=0,
        tiled=True,
    ).astype(jnp.float32)
    first_pull = jax.vjp(layer_norm, pre_first, g1, b1)[1]
    d_pre1, d_gain1, d_bias1 = first_pull(d_normed)
    d_attn_low = d_pre1.astype(jnp.bfloat16)
    d_wo = jnp.dot(ctx_low.T, d_attn_low, preferred_element_type=jnp.float32)
    d_ctx = (
        jnp.dot(d_attn_low, wo.T, preferred_element_type=jnp.float32)
        .astype(jnp.bfloat16)
        .reshape(rows, HEADS, HEAD_DIM)
    )
    query, keys, values = split_heads(qkv_low, width)
    probs = jnp.exp(scores_of(query, keys, same, decay) - log_total)
    probs_low = probs.astype(jnp.bfloat16)
    d_values = jnp.einsum("hqk,qhe->khe", probs_low, d_ctx, preferred_element_type=jnp.float32)
    d_probs = jnp.einsum("qhe,khe->hqk", d_ctx, values, preferred_element_type=jnp.float32)
    d_scores = (probs * (d_probs - jnp.sum(probs * d_probs, axis=-1, keepdims=True))).astype(
        jnp.bfloat16
    )
    d_query = jnp.einsum(
        "hqk,khe->qhe", d_scores, keys, preferred_element_type=jnp.float32
    ) * HEAD_DIM ** (-0.5)
    d_keys = jnp.einsum(
        "hqk,qhe->khe", d_scores, query, preferred_element_type=jnp.float32
    ) * HEAD_DIM ** (-0.5)
    d_qkv = jnp.concatenate(
        [d_query.reshape(rows, width), d_keys.reshape(rows, width), d_values.reshape(rows, width)],
        axis=1,
    ).astype(jnp.bfloat16)
    d_wqkv = jnp.dot(x_low.T, d_qkv, preferred_element_type=jnp.float32)
    d_input = d_pre1 + jnp.dot(d_qkv, wqkv.T, preferred_element_type=jnp.float32)
    return (d_input, d_wqkv, d_wo, d_gain1, d_bias1, d_up, d_down, d_gain2, d_bias2)


def shards(
    x_in,
    bucket,
    lengths,
    qkv_weight,
    out_weight,
    norm_gain1,
    norm_bias1,
    up_weight,
    down_weight,
    norm_gain2,
    norm_bias2,
    cotangent,
):
    rows = x_in.shape[0]
    seg = segments(bucket[0], lengths[0], rows, SHORT)
    same = seg[:, None] == seg[None, :]
    decay = alibi(rows, HEADS)
    layer_in = x_in
    outputs = []
    kept = []
    for layer in range(LAYERS):
        layer_in, keep = forward_layer(
            layer_in,
            qkv_weight[layer],
            out_weight[layer],
            norm_gain1[layer],
            norm_bias1[layer],
            up_weight[layer],
            down_weight[layer],
            norm_gain2[layer],
            norm_bias2[layer],
            same,
            decay,
        )
        outputs.append(layer_in)
        kept.append(keep)
    grad = cotangent.astype(jnp.float32)
    found = [None] * LAYERS
    for layer in reversed(range(LAYERS)):
        grad, d_wqkv, d_wo, d_gain1, d_bias1, d_up, d_down, d_gain2, d_bias2 = backward_layer(
            grad,
            kept[layer],
            qkv_weight[layer],
            out_weight[layer],
            norm_gain1[layer],
            norm_bias1[layer],
            up_weight[layer],
            down_weight[layer],
            norm_gain2[layer],
            norm_bias2[layer],
            same,
            decay,
        )
        d_wqkv, d_wo, d_gain1, d_bias1, d_gain2, d_bias2 = lax.psum(
            (d_wqkv, d_wo, d_gain1, d_bias1, d_gain2, d_bias2), ("dp", "tensor")
        )
        d_up, d_down = (
            lax.psum_scatter(
                d_up.astype(jnp.bfloat16), "dp", scatter_dimension=0, tiled=True
            ).astype(jnp.float32),
            lax.psum_scatter(
                d_down.astype(jnp.bfloat16), "dp", scatter_dimension=1, tiled=True
            ).astype(jnp.float32),
        )
        found[layer] = (d_wqkv, d_wo, d_gain1, d_bias1, d_up, d_down, d_gain2, d_bias2)
    stacked = [jnp.stack([found[layer][index] for layer in range(LAYERS)]) for index in range(8)]
    qkv_grad, out_grad, gain1_grad, bias1_grad, up_grad, down_grad, gain2_grad, bias2_grad = stacked
    activations = jnp.stack(outputs)
    return (
        activations,
        grad,
        qkv_grad,
        out_grad,
        gain1_grad,
        bias1_grad,
        up_grad,
        down_grad,
        gain2_grad,
        bias2_grad,
    )


def solution(mesh):
    in_specs = (
        P(("dp", "tensor"), None),
        P(("dp", "tensor")),
        P(("dp", "tensor"), None),
        P(),
        P(),
        P(),
        P(),
        P(None, None, None, "tensor"),
        P(None, "tensor", None),
        P(),
        P(),
        P(("dp", "tensor"), None),
    )
    out_specs = (
        P(None, ("dp", "tensor"), None),
        P(("dp", "tensor"), None),
        P(),
        P(),
        P(),
        P(),
        P(None, "dp", None, "tensor"),
        P(None, "tensor", "dp"),
        P(),
        P(),
    )
    return jax.shard_map(shards, mesh=mesh, in_specs=in_specs, out_specs=out_specs, check_vma=False)
```

profile of v0, /device:TPU:0, one launch (start us, length us, event | category | flops | bytes accessed | tf_op | source)
XLA Modules:
  0.0 1206.9 jit_solution(10613801410674038543)
XLA Ops:
  32.5 7.0 fusion.100
  41.4 57.2 %all-gather.5.cloned.1.call-done = bf16[2048,768]{1,0:T(8,128)(2,1)} async-done(((bf16[512,768]{1,0:T(8,128)(2,1)}), bf16[2048,768]{1,0:T(8,128)(2,1)}) %all-gather.5.cloned.1.call-update) | async-done | bytes 3145744 | tf_op jit(solution)/shard_map/all_gather | solution.py:84
  98.6 7.7 fusion.107
  117.8 58.3 %reduce-scatter.7.cloned.1.call-done = bf16[512,768]{1,0:T(8,128)(2,1)} async-done(((bf16[2048,768]{1,0:T(8,128)(2,1)}), bf16[512,768]{1,0:T(8,128)(2,1)}) %reduce-scatter.7.cloned.1.call-update) | async-done | bytes 786448 | tf_op jit(solution)/shard_map/reduce_scatter | solution.py:87
  205.4 60.0 %all-gather.7.cloned.1.call-done = bf16[2048,768]{1,0:T(8,128)(2,1)} async-done(((bf16[512,768]{1,0:T(8,128)(2,1)}), bf16[2048,768]{1,0:T(8,128)(2,1)}) %all-gather.7.cloned.1.call-update) | async-done | bytes 3145744 | tf_op jit(solution)/shard_map/all_gather | solution.py:84
  265.3 7.7 fusion.108
  283.7 59.0 %reduce-scatter.9.cloned.1.call-done = bf16[512,768]{1,0:T(8,128)(2,1)} async-done(((bf16[2048,768]{1,0:T(8,128)(2,1)}), bf16[512,768]{1,0:T(8,128)(2,1)}) %reduce-scatter.9.cloned.1.call-update) | async-done | bytes 786448 | tf_op jit(solution)/shard_map/reduce_scatter | solution.py:87
  350.1 63.4 %all-gather.9.cloned.1.call-done = bf16[2048,768]{1,0:T(8,128)(2,1)} async-done(((bf16[512,768]{1,0:T(8,128)(2,1)}), bf16[2048,768]{1,0:T(8,128)(2,1)}) %all-gather.9.cloned.1.call-update) | async-done | bytes 3145744 | tf_op jit(solution)/shard_map/all_gather | solution.py:128
  413.6 12.0 fusion.25
  436.7 59.0 %reduce-scatter.11.cloned.1.call-done = bf16[512,768]{1,0:T(8,128)(2,1)} async-done(((bf16[2048,768]{1,0:T(8,128)(2,1)}), bf16[512,768]{1,0:T(8,128)(2,1)}) %reduce-scatter.11.cloned.1.call-update) | async-done | bytes 786448 | tf_op jit(solution)/shard_map/reduce_scatter | solution.py:134
  502.1 7.7 fusion.51
  509.8 9.2 multiply_reduce_fusion.1
  536.6 63.6 %all-gather.11.cloned.1.call-done = bf16[2048,768]{1,0:T(8,128)(2,1)} async-done(((bf16[512,768]{1,0:T(8,128)(2,1)}), bf16[2048,768]{1,0:T(8,128)(2,1)}) %all-gather.11.cloned.1.call-update) | async-done | bytes 3145744 | tf_op jit(solution)/shard_map/all_gather | solution.py:128
  600.3 12.6 %fusion.24 = (f32[2048,768]{1,0:T(8,128)S(1)}, f32[2048,768]{1,0:T(8,128)S(1)}) fusion(f32[2048,1536]{1,0:T(8,128)} %copy-done.8, bf16[2048,768]{1,0:T(8,128)(2,1)} %all-gather.11.cloned.1.call-done, bf16[2,768,768]{2,1,0:T(8,128)(2,1)} %param.20), kind=kOutput, calls=%fused_computation.69 | convolution fusion | flops 2456813568 | bytes 29491200 | tf_op jit(solution)/shard_map/dot_general | solution.py:129
  630.9 12.0 convolution_convert_fusion.2
  664.5 9.3 convolution_convert_fusion.3
  691.0 10.9 multiply_reduce_fusion
  704.0 7.0 multiply_convert_fusion
  728.1 35.8 %reduce-scatter.15.cloned.1.call-done = bf16[768,96]{0,1:T(8,128)(2,1)} async-done(((bf16[768,768]{0,1:T(8,128)(2,1)}), bf16[768,96]{0,1:T(8,128)(2,1)}) %reduce-scatter.15.cloned.1.call-update) | async-done | bytes 147472 | tf_op jit(solution)/shard_map/reduce_scatter | solution.py:233
  765.8 88.5 %all-reduce.14.cloned.1.call-done = (bf16[768,2,768]{2,1,0:T(2,128)(2,1)}, bf16[768,2,768]{2,1,0:T(2,128)(2,1)}) async-done(((bf16[768,2,768]{2,1,0:T(2,128)(2,1)}, bf16[768,2,768]{2,1,0:T(2,128)(2,1)}), (bf16[768,2,768]{2,1,0:T(2,128)(2,1)}, bf16[768,2,768]{2,1,0:T(2,128)(2,1)})) %all-reduce.14.cloned.1.call-update) | async-done | bytes 4718608
  858.5 41.8 %all-reduce.6 = (f32[1,768]{1,0:T(1,128)S(1)}, f32[1,768]{1,0:T(1,128)S(1)}, f32[1,768]{1,0:T(1,128)S(1)}, f32[1,768]{1,0:T(1,128)S(1)}, f32[1,768]{1,0:T(1,128)...) all-reduce(f32[1,768]{1,0:T(1,128)S(1)} %stack.101, ...), channel_id=1, replica_groups=mesh['dp'=8,'tensor'=4] {'dp','tensor'}, use_global_device_ids=true, to_apply=%region_35.36 | all-reduce | flops 6144 | bytes 49152 | tf_op jit(solution)/shard_map/psum | solution.py:226
  908.2 260.8 %all-reduce.12.cloned.1.call-done = (f32[1,768,2304]{1,2,0:T(8,128)}, f32[1,768,2304]{1,2,0:T(8,128)}, f32[1,768,768]{2,1,0:T(8,128)}, f32[1,768,768]{2,1,0:T(8,128)}) async-done(((f32[1,768,2304]{1,2,0:T(8,128)}, f32[1,768,2304]{1,2,0:T(8,128)}, f32[1,768,768]{2,1,0:T(8,128)}, f32[1,768,768]{2,1,0:T(8,128)}), (f32[1,768,2304]{1,2,0:T(8,128)}, f32[1,768,2304]{1,2,0:T(8,128)}, f32[1,768,768]{2,1,0:T(8,128)}, ...) | async-done | bytes 18874384 | tf_op jit(solution)/shard_map/psum | solution.py:226
  1169.0 11.0 pad_maximum_fusion
  1179.9 15.4 %copy.101 = f32[2,768,2304]{2,1,0:T(8,128)} copy(f32[2,768,2304]{1,2,0:T(8,128)} %pad_maximum_fusion) | data formatting | bytes 28311552
  (326 shorter events, 212.5 us)
Async XLA Ops:
  7.2 91.5 %all-gather.5.cloned.1.call-start = ((), (), s32[]{:S(2)}) async-start(), calls=%async_computation.6 | async-start | bytes 3932160 | tf_op jit(solution)/shard_map/all_gather | solution.py:84
  29.9 146.2 %copy-start.2 = (f32[512,768]{1,0:T(8,128)}, f32[512,768]{1,0:T(8,128)S(1)}, u32[]{:S(2)}) copy-start(f32[512,768]{1,0:T(8,128)S(1)} %get-tuple-element.112) | copy-start | bytes 4718596
  30.0 146.2 %copy-start.53 = (f32[512]{0:T(512)}, f32[512]{0:T(512)S(1)}, u32[]{:S(2)}) copy-start(f32[512]{0:T(512)S(1)} %broadcast_multiply_fusion.3) | copy-start | bytes 6148
  31.0 145.1 %copy-start.55 = (f32[512]{0:T(512)}, f32[512]{0:T(512)S(1)}, u32[]{:S(2)}) copy-start(f32[512]{0:T(512)S(1)} %fusion.80) | copy-start | bytes 6148
  31.1 145.1 %copy-start.51 = (f32[768]{0:T(1024)}, f32[768]{0:T(1024)S(1)}, u32[]{:S(2)}) copy-start(f32[768]{0:T(1024)S(1)} %get-tuple-element.122) | copy-start | bytes 9220
  32.3 143.8 %reduce-scatter.7.cloned.1.call-start = ((), (), s32[]{:S(2)}) async-start(), calls=%async_computation.7 | async-start | bytes 3932160 | tf_op jit(solution)/shard_map/reduce_scatter | solution.py:87
  117.0 148.3 %all-gather.7.cloned.1.call-start = ((), (), s32[]{:S(2)}) async-start(), calls=%async_computation.8 | async-start | bytes 3932160 | tf_op jit(solution)/shard_map/all_gather | solution.py:84
  117.8 81.4 %copy-start.59 = (f32[768]{0:T(1024)}, f32[768]{0:T(1024)S(1)}, u32[]{:S(2)}) copy-start(f32[768]{0:T(1024)S(1)} %get-tuple-element.65) | copy-start | bytes 9220
  201.7 141.1 %reduce-scatter.9.cloned.1.call-start = ((), (), s32[]{:S(2)}) async-start(), calls=%async_computation.9 | async-start | bytes 3932160 | tf_op jit(solution)/shard_map/reduce_scatter | solution.py:87
  283.7 129.9 %all-gather.9.cloned.1.call-start = ((), (), s32[]{:S(2)}) async-start(), calls=%async_computation.10 | async-start | bytes 3932160 | tf_op jit(solution)/shard_map/all_gather | solution.py:128
  349.9 145.8 %reduce-scatter.11.cloned.1.call-start = ((), (), s32[]{:S(2)}) async-start(), calls=%async_computation.11 | async-start | bytes 3932160 | tf_op jit(solution)/shard_map/reduce_scatter | solution.py:134
  413.6 16.6 %copy-start.40 = (bf16[96,8,2,768]{3,1,2,0:T(8,128)(2,1)S(1)}, bf16[96,8,2,768]{3,1,2,0:T(8,128)(2,1)}, u32[]{:S(2)}) copy-start(bf16[96,8,2,768]{3,1,2,0:T(8,128)(2,1)} %copy.112) | copy-start | bytes 7077892
  436.6 163.6 %all-gather.11.cloned.1.call-start = ((), (), s32[]{:S(2)}) async-start(), calls=%async_computation.12 | async-start | bytes 3932160 | tf_op jit(solution)/shard_map/all_gather | solution.py:128
  502.1 16.9 %slice-start.3 = ((s8[12582912]{0:T(1024)(128)(4,1)}), s8[4194304]{0:T(1024)(128)(4,1)S(1)}, s32[]{:S(2)}) async-start(s8[12582912]{0:T(1024)(128)(4,1)} %bitcast.151), calls=%async_computation.21 | async-start | bytes 8388608
  502.1 16.9 %slice-start.4 = ((s8[12582912]{0:T(1024)(128)(4,1)}), s8[4194304]{0:T(1024)(128)(4,1)S(1)}, s32[]{:S(2)}) async-start(s8[12582912]{0:T(1024)(128)(4,1)} %bitcast.151), calls=%async_computation.22 | async-start | bytes 8388608
  536.6 146.5 %reduce-scatter.13.cloned.1.call-start = ((), (), s32[]{:S(2)}) async-start(), calls=%async_computation.13 | async-start | bytes 3932160 | tf_op jit(solution)/shard_map/reduce_scatter | solution.py:134
  600.3 17.3 %copy-start.39 = (bf16[96,8,2,768]{3,1,2,0:T(8,128)(2,1)S(1)}, bf16[96,8,2,768]{3,1,2,0:T(8,128)(2,1)}, u32[]{:S(2)}) copy-start(bf16[96,8,2,768]{3,1,2,0:T(8,128)(2,1)} %copy.111) | copy-start | bytes 7077892
  624.0 104.1 %reduce-scatter.17.cloned.1.call-start = ((), (), s32[]{:S(2)}) async-start(), calls=%async_computation.15 | async-start | bytes 1327104 | tf_op jit(solution)/shard_map/reduce_scatter | solution.py:233
  630.6 133.3 %reduce-scatter.15.cloned.1.call-start = ((), (), s32[]{:S(2)}) async-start(), calls=%async_computation.14 | async-start | bytes 1327104 | tf_op jit(solution)/shard_map/reduce_scatter | solution.py:233
  655.5 198.8 %all-reduce.14.cloned.1.call-start = ((), (), s32[]{:S(2)}) async-start(), calls=%async_computation.17 | async-start | bytes 9437184
  679.8 489.2 %all-reduce.12.cloned.1.call-start = ((), (), s32[]{:S(2)}) async-start(), calls=%async_computation.16 | async-start | bytes 37748736 | tf_op jit(solution)/shard_map/psum | solution.py:226
  728.0 174.6 %copy-start.20 = (f32[512,768]{1,0:T(8,128)S(1)}, f32[512,768]{1,0:T(8,128)}, u32[]{:S(2)}) copy-start(f32[512,768]{1,0:T(8,128)} %copy-done.18) | copy-start | bytes 4718596
  728.0 174.6 %copy-start.36 = (bf16[12,64,512]{2,1,0:T(8,128)(2,1)S(1)}, bf16[12,64,512]{2,1,0:T(8,128)(2,1)}, u32[]{:S(2)}) copy-start(bf16[12,64,512]{2,1,0:T(8,128)(2,1)} %copy-done.35) | copy-start | bytes 2359300
  728.0 174.6 %copy-start.45 = (bf16[12,64,512]{2,1,0:T(8,128)(2,1)S(1)}, bf16[12,64,512]{2,1,0:T(8,128)(2,1)}, u32[]{:S(2)}) copy-start(bf16[12,64,512]{2,1,0:T(8,128)(2,1)} %copy-done.44) | copy-start | bytes 2359300
  (81 other events, 314.6 us)
Sparse Core Ops, SparseCore 0:
  32.4 66.1 all-gather.4
  117.2 58.8 reduce-scatter.6
  201.8 63.5 all-gather.6
  283.8 58.8 reduce-scatter.8
  350.0 63.5 all-gather.8
  436.7 58.8 reduce-scatter.10
  536.7 63.5 all-gather.10
  624.2 58.8 reduce-scatter.12
  686.9 36.8 reduce-scatter.16
  727.2 36.7 reduce-scatter.14
  767.3 86.9 all-reduce.13
  862.3 306.5 all-reduce.11
where the time goes:
time: 1220 us; the launch traced here: 1210 us
  waiting for transfers between devices  809 us (66%)
  matrix products  182 us (15%)
  local copies, waits for them, and re-layouts  85.4 us (7%)
  other arithmetic  69 us (6%)
  blocking collectives  41.8 us (3%)
  between operations  17.3 us (1%)
    psum x1, waiting for transfers between devices, shards(): lax.psum((d_wqkv, d_wo, d_gain1, d_bias1, d_gain2, d_bias2), ('dp', 'tens...  261 us
    all_gather x2, waiting for transfers between devices, backward_layer(): lax.all_gather(d_pre2.astype(jnp.bfloat16), 'tensor', axis=0, tiled=True)  127 us
    reduce_scatter x2, waiting for transfers between devices, forward_layer(): lax.psum_scatter(jnp.dot(act_low, wdown, preferred_element_type=jnp.float...  117 us
    all_gather x2, waiting for transfers between devices, forward_layer(): gathered = lax.all_gather(normed_low, 'tensor', axis=0, tiled=True)  117 us
    unnamed x13, waiting for transfers between devices  88.7 us
    reduce_scatter x2, waiting for transfers between devices, backward_layer(): lax.psum_scatter(jnp.dot(d_joined, up_flat.T, preferred_element_type=jnp....  62.3 us
    unnamed x190, local copies, waits for them, and re-layouts  56 us
    psum x1, blocking collectives, shards(): lax.psum((d_wqkv, d_wo, d_gain1, d_bias1, d_gain2, d_bias2), ('dp', 'tens...  41.8 us
  transfers between devices with their start and end apart: 12, of which 11 were waited for; matrix products, arithmetic and copies ran while one was open for 10% of the time, Pallas kernels for 0%

commit v1 on v0

--- a/solution.py
+++ b/solution.py
@@ -10,6 +10,21 @@
 eps_norm = 1e-05
 gelu_coef = 0.7978845608028654
 masked_score = -1e30
+
+
+def sheets_refer(inputs, in_dim):
+    a_name = "tensor"
+    carry = lax.psum(1, a_name)
+    latest = lax.axis_index(a_name)
+    local_next, everything = (carry, latest)
+    big, parts_out = (inputs, 1)
+    while parts_out < local_next:
+        mid_arr = lax.ppermute(big, a_name, [(j, j ^ parts_out) for j in range(local_next)])
+        clean = jnp.concatenate([big, mid_arr], in_dim)
+        even = jnp.concatenate([mid_arr, big], axis=in_dim)
+        big = jnp.where(everything & parts_out == 0, clean, even)
+        parts_out = 2 * parts_out
+    return big
 
 
 def segments(bucket_one, lens, rows_dev, short_len):
@@ -125,7 +140,7 @@
     up_flat = wup.reshape(width, -1)
     second_pull = jax.vjp(layer_norm, pre_second, g2, b2)[1]
     d_pre2, d_gain2, d_bias2 = second_pull(grad_out)
-    grad_rows = lax.all_gather(d_pre2.astype(jnp.bfloat16), "tensor", axis=0, tiled=True)
+    grad_rows = sheets_refer(d_pre2.astype(jnp.bfloat16), 0)
     d_act = jnp.dot(grad_rows, wdown.T, preferred_element_type=jnp.float32)
     d_down = jnp.dot(act_low.T, grad_rows, preferred_element_type=jnp.float32)
     geglu_pull = jax.vjp(geglu, joined)[1]

time: 1220 us -> 1280 us (1.049)
  waiting for transfers between devices: 809 us -> 853 us
    ppermute x0 -> x4, waiting for transfers between devices: none -> 171 us  [sheets_refer(): lax.ppermute(big, a_name, [(j, j ^ parts_out) for j in range(local_next)])]
    all_gather x2 -> x0, waiting for transfers between devices: 127 us -> none  [backward_layer(): lax.all_gather(d_pre2.astype(jnp.bfloat16), 'tensor', axis=0, tiled=True)]
    unnamed x190 -> x188, local copies, waits for them, and re-layouts: 56 us -> 49.6 us
    unnamed x13 -> x11, waiting for transfers between devices: 88.7 us -> 88.7 us
  transfers between devices with their start and end apart: 12 -> 14, of which waited for: 11 -> 13; matrix products, arithmetic and copies ran while one was open for 10% -> 10% of each run, Pallas kernels for 0% -> 0%
where the time goes in v1:
time: 1280 us; the launch traced here: 1270 us
  waiting for transfers between devices  853 us (67%)
  matrix products  194 us (15%)
  local copies, waits for them, and re-layouts  79.3 us (6%)
  other arithmetic  73.6 us (6%)
  blocking collectives  41.8 us (3%)
  between operations  16.9 us (1%)
    psum x1, waiting for transfers between devices, shards(): lax.psum((d_wqkv, d_wo, d_gain1, d_bias1, d_gain2, d_bias2), ('dp', 'tens...  261 us
    ppermute x4, waiting for transfers between devices, sheets_refer(): lax.ppermute(big, a_name, [(j, j ^ parts_out) for j in range(local_next)])  171 us
    reduce_scatter x2, waiting for transfers between devices, forward_layer(): lax.psum_scatter(jnp.dot(act_low, wdown, preferred_element_type=jnp.float...  117 us
    all_gather x2, waiting for transfers between devices, forward_layer(): gathered = lax.all_gather(normed_low, 'tensor', axis=0, tiled=True)  117 us
    unnamed x11, waiting for transfers between devices  88.7 us
    reduce_scatter x2, waiting for transfers between devices, backward_layer(): lax.psum_scatter(jnp.dot(d_joined, up_flat.T, preferred_element_type=jnp....  63 us
    unnamed x188, local copies, waits for them, and re-layouts  49.6 us
    psum x1, blocking collectives, shards(): lax.psum((d_wqkv, d_wo, d_gain1, d_bias1, d_gain2, d_bias2), ('dp', 'tens...  41.8 us
  transfers between devices with their start and end apart: 14, of which 13 were waited for; matrix products, arithmetic and copies ran while one was open for 10% of the time, Pallas kernels for 0%

profile of v1, /device:TPU:0, one launch (start us, length us, event | category | flops | bytes accessed | tf_op | source)
XLA Modules:
  0.0 1267.8 jit_solution(17815977652460607213)
XLA Ops:
  41.6 57.0 %all-gather.3.cloned.1.call-done = bf16[2048,768]{1,0:T(8,128)(2,1)} async-done(((bf16[512,768]{1,0:T(8,128)(2,1)}), bf16[2048,768]{1,0:T(8,128)(2,1)}) %all-gather.3.cloned.1.call-update) | async-done | bytes 3145744 | tf_op jit(solution)/shard_map/all_gather | solution.py:99
  117.7 58.3 %reduce-scatter.7.cloned.1.call-done = bf16[512,768]{1,0:T(8,128)(2,1)} async-done(((bf16[2048,768]{1,0:T(8,128)(2,1)}), bf16[512,768]{1,0:T(8,128)(2,1)}) %reduce-scatter.7.cloned.1.call-update) | async-done | bytes 786448 | tf_op jit(solution)/shard_map/reduce_scatter | solution.py:102
  205.4 59.9 %all-gather.5.cloned.1.call-done = bf16[2048,768]{1,0:T(8,128)(2,1)} async-done(((bf16[512,768]{1,0:T(8,128)(2,1)}), bf16[2048,768]{1,0:T(8,128)(2,1)}) %all-gather.5.cloned.1.call-update) | async-done | bytes 3145744 | tf_op jit(solution)/shard_map/all_gather | solution.py:99
  284.1 58.6 %reduce-scatter.9.cloned.1.call-done = bf16[512,768]{1,0:T(8,128)(2,1)} async-done(((bf16[2048,768]{1,0:T(8,128)(2,1)}), bf16[512,768]{1,0:T(8,128)(2,1)}) %reduce-scatter.9.cloned.1.call-update) | async-done | bytes 786448 | tf_op jit(solution)/shard_map/reduce_scatter | solution.py:102
  350.8 18.4 %collective-permute-done = bf16[512,768]{1,0:T(8,128)(2,1)} collective-permute-done((bf16[512,768]{1,0:T(8,128)(2,1)}, bf16[512,768]{1,0:T(8,128)(2,1)}, u32[]{:S(2)}, u32[]{:S(2)}) %collective-permute-start) | collective-permute-done | bytes 786464 | tf_op jit(solution)/shard_map/ppermute | solution.py:22
  375.4 67.6 %collective-permute-done.1 = bf16[1024,768]{1,0:T(8,128)(2,1)} collective-permute-done((bf16[1024,768]{1,0:T(8,128)(2,1)}, bf16[1024,768]{1,0:T(8,128)(2,1)}, u32[]{:S(2)}, u32[]{:S(2)}) %collective-permute-start.1) | collective-permute-done | bytes 1572896 | tf_op jit(solution)/shard_map/ppermute | solution.py:22
  443.0 15.2 %fusion.25 = (f32[2048,768]{1,0:T(8,128)S(1)}, f32[2048,768]{1,0:T(8,128)}) fusion(f32[2048,1536]{1,0:T(8,128)} %copy-done.9, bf16[2,768,768]{2,1,0:T(8,128)(2,1)} %param.20, bf16[1024,768]{1,0:T(8,128)(2,1)} %collective-permute-done.1, bf16[1024,768]{1,0:T(8,128)(2,1)} %maximum_select_fusion.2, pred[]{:T(512)S(6)} %eq.52), kind=kOutput, calls=%fused_computation.72 | convolution fusion | flops 2470969344 | bytes 29491200 | tf_op jit(solution)/shard_map/dot_general | solution.py:144
  460.7 8.3 convolution_convert_fusion.7
  469.1 60.5 %reduce-scatter.11.cloned.1.call-done = bf16[512,768]{1,0:T(8,128)(2,1)} async-done(((bf16[2048,768]{1,0:T(8,128)(2,1)}), bf16[512,768]{1,0:T(8,128)(2,1)}) %reduce-scatter.11.cloned.1.call-update) | async-done | bytes 786448 | tf_op jit(solution)/shard_map/reduce_scatter | solution.py:149
  543.7 9.2 multiply_reduce_fusion.1
  570.6 18.1 %collective-permute-done.2 = bf16[512,768]{1,0:T(8,128)(2,1)S(1)} collective-permute-done((bf16[512,768]{1,0:T(8,128)(2,1)S(1)}, bf16[512,768]{1,0:T(8,128)(2,1)S(1)}, u32[]{:S(2)}, u32[]{:S(2)}) %collective-permute-start.2) | collective-permute-done | bytes 786464 | tf_op jit(solution)/shard_map/ppermute | solution.py:22
  592.2 67.3 %collective-permute-done.3 = bf16[1024,768]{1,0:T(8,128)(2,1)S(1)} collective-permute-done((bf16[1024,768]{1,0:T(8,128)(2,1)S(1)}, bf16[1024,768]{1,0:T(8,128)(2,1)S(1)}, u32[]{:S(2)}, u32[]{:S(2)}) %collective-permute-start.3) | collective-permute-done | bytes 1572896 | tf_op jit(solution)/shard_map/ppermute | solution.py:22
  659.5 14.6 %fusion.24 = (f32[2048,768]{1,0:T(8,128)}, f32[2048,768]{1,0:T(8,128)}) fusion(f32[2048,1536]{1,0:T(8,128)} %copy-done.8, bf16[2,768,768]{2,1,0:T(8,128)(2,1)S(1)} %copy-done.72, bf16[1024,768]{1,0:T(8,128)(2,1)S(1)} %collective-permute-done.3, bf16[1024,768]{1,0:T(8,128)(2,1)S(1)} %maximum_select_fusion.3, pred[]{:T(512)S(6)} %eq.52), kind=kOutput, calls=%fused_computation.71 | convolution fusion | flops 2470969344 | bytes 29491200 | tf_op jit(solution)/shard_map/dot_general | solution.py:144
  674.1 9.5 convolution_convert_fusion.6
  683.7 7.8 convolution_convert_fusion.8
  691.5 12.0 convolution_convert_fusion.2
  726.3 9.3 convolution_convert_fusion.3
  752.0 10.8 multiply_reduce_fusion
  790.4 34.8 %reduce-scatter.15.cloned.1.call-done = bf16[768,96]{0,1:T(8,128)(2,1)} async-done(((bf16[768,768]{0,1:T(8,128)(2,1)}), bf16[768,96]{0,1:T(8,128)(2,1)}) %reduce-scatter.15.cloned.1.call-update) | async-done | bytes 147472 | tf_op jit(solution)/shard_map/reduce_scatter | solution.py:248
  827.0 88.5 %all-reduce.14.cloned.1.call-done = (bf16[768,2,768]{2,1,0:T(2,128)(2,1)}, bf16[768,2,768]{2,1,0:T(2,128)(2,1)}) async-done(((bf16[768,2,768]{2,1,0:T(2,128)(2,1)}, bf16[768,2,768]{2,1,0:T(2,128)(2,1)}), (bf16[768,2,768]{2,1,0:T(2,128)(2,1)}, bf16[768,2,768]{2,1,0:T(2,128)(2,1)})) %all-reduce.14.cloned.1.call-update) | async-done | bytes 4718608
  919.7 41.8 %all-reduce.6 = (f32[1,768]{1,0:T(1,128)S(1)}, f32[1,768]{1,0:T(1,128)S(1)}, f32[1,768]{1,0:T(1,128)S(1)}, f32[1,768]{1,0:T(1,128)S(1)}, f32[1,768]{1,0:T(1,128)...) all-reduce(f32[1,768]{1,0:T(1,128)S(1)} %stack.101, ...), channel_id=1, replica_groups=mesh['dp'=8,'tensor'=4] {'dp','tensor'}, use_global_device_ids=true, to_apply=%region_35.36 | all-reduce | flops 6144 | bytes 49152 | tf_op jit(solution)/shard_map/psum | solution.py:241
  969.3 260.8 %all-reduce.12.cloned.1.call-done = (f32[1,768,2304]{1,2,0:T(8,128)}, f32[1,768,2304]{1,2,0:T(8,128)}, f32[1,768,768]{2,1,0:T(8,128)}, f32[1,768,768]{2,1,0:T(8,128)}) async-done(((f32[1,768,2304]{1,2,0:T(8,128)}, f32[1,768,2304]{1,2,0:T(8,128)}, f32[1,768,768]{2,1,0:T(8,128)}, f32[1,768,768]{2,1,0:T(8,128)}), (f32[1,768,2304]{1,2,0:T(8,128)}, f32[1,768,2304]{1,2,0:T(8,128)}, f32[1,768,768]{2,1,0:T(8,128)}, ...) | async-done | bytes 18874384 | tf_op jit(solution)/shard_map/psum | solution.py:241
  1230.2 11.0 pad_maximum_fusion
  1241.1 15.4 %copy.101 = f32[2,768,2304]{2,1,0:T(8,128)} copy(f32[2,768,2304]{1,2,0:T(8,128)} %pad_maximum_fusion) | data formatting | bytes 28311552
  (328 shorter events, 236.1 us)
Async XLA Ops:
  7.2 91.4 %all-gather.3.cloned.1.call-start = ((), (), s32[]{:S(2)}) async-start(), calls=%async_computation.6 | async-start | bytes 3932160 | tf_op jit(solution)/shard_map/all_gather | solution.py:99
  29.9 146.2 %copy-start.2 = (f32[512,768]{1,0:T(8,128)}, f32[512,768]{1,0:T(8,128)S(1)}, u32[]{:S(2)}) copy-start(f32[512,768]{1,0:T(8,128)S(1)} %get-tuple-element.112) | copy-start | bytes 4718596
  29.9 146.1 %copy-start.53 = (f32[512]{0:T(512)}, f32[512]{0:T(512)S(1)}, u32[]{:S(2)}) copy-start(f32[512]{0:T(512)S(1)} %broadcast_multiply_fusion.3) | copy-start | bytes 6148
  31.0 145.1 %copy-start.55 = (f32[512]{0:T(512)}, f32[512]{0:T(512)S(1)}, u32[]{:S(2)}) copy-start(f32[512]{0:T(512)S(1)} %fusion.80) | copy-start | bytes 6148
  31.0 145.0 %copy-start.51 = (f32[768]{0:T(1024)}, f32[768]{0:T(1024)S(1)}, u32[]{:S(2)}) copy-start(f32[768]{0:T(1024)S(1)} %get-tuple-element.122) | copy-start | bytes 9220
  32.2 143.8 %reduce-scatter.7.cloned.1.call-start = ((), (), s32[]{:S(2)}) async-start(), calls=%async_computation.7 | async-start | bytes 3932160 | tf_op jit(solution)/shard_map/reduce_scatter | solution.py:102
  117.0 148.3 %all-gather.5.cloned.1.call-start = ((), (), s32[]{:S(2)}) async-start(), calls=%async_computation.8 | async-start | bytes 3932160 | tf_op jit(solution)/shard_map/all_gather | solution.py:99
  201.6 141.1 %reduce-scatter.9.cloned.1.call-start = ((), (), s32[]{:S(2)}) async-start(), calls=%async_computation.9 | async-start | bytes 3932160 | tf_op jit(solution)/shard_map/reduce_scatter | solution.py:102
  283.7 245.9 %reduce-scatter.11.cloned.1.call-start = ((), (), s32[]{:S(2)}) async-start(), calls=%async_computation.10 | async-start | bytes 3932160 | tf_op jit(solution)/shard_map/reduce_scatter | solution.py:149
  349.8 19.4 %collective-permute-start = (bf16[512,768]{1,0:T(8,128)(2,1)}, bf16[512,768]{1,0:T(8,128)(2,1)}, u32[]{:S(2)}, u32[]{:S(2)}) collective-permute-start(bf16[512,768]{1,0:T(8,128)(2,1)} %add_convert_fusion.7), channel_id=1, source_target_pairs={{0,1},{1,0},{2,3},{3,2},{4,5},{5,4},{6,7},{7,6},{8,9},{9,8},{10,11... | collective-permute-start | bytes 2359304 | tf_op jit(solution)/shard_map/ppermute | solution.py:22
  372.7 70.3 %collective-permute-start.1 = (bf16[1024,768]{1,0:T(8,128)(2,1)}, bf16[1024,768]{1,0:T(8,128)(2,1)}, u32[]{:S(2)}, u32[]{:S(2)}) collective-permute-start(bf16[1024,768]{1,0:T(8,128)(2,1)} %maximum_select_fusion.2), channel_id=1, source_target_pairs={{0,2},{1,3},{2,0},{3,1},{4,6},{5,7},{6,4},{7,5},{8,10},{9,11},{10,... | collective-permute-start | bytes 4718600 | tf_op jit(solution)/shard_map/ppermute | solution.py:22
  375.4 85.4 %copy-start.39 = (bf16[96,8,2,768]{3,1,2,0:T(8,128)(2,1)S(1)}, bf16[96,8,2,768]{3,1,2,0:T(8,128)(2,1)}, u32[]{:S(2)}) copy-start(bf16[96,8,2,768]{3,1,2,0:T(8,128)(2,1)} %copy.112) | copy-start | bytes 7077892
  469.1 275.1 %reduce-scatter.13.cloned.1.call-start = ((), (), s32[]{:S(2)}) async-start(), calls=%async_computation.11 | async-start | bytes 3932160 | tf_op jit(solution)/shard_map/reduce_scatter | solution.py:149
  568.2 91.3 %copy-start.72 = (bf16[2,768,768]{2,1,0:T(8,128)(2,1)S(1)}, bf16[2,768,768]{2,1,0:T(8,128)(2,1)}, u32[]{:S(2)}) copy-start(bf16[2,768,768]{2,1,0:T(8,128)(2,1)} %param.20) | copy-start | bytes 7077892
  569.5 19.2 %collective-permute-start.2 = (bf16[512,768]{1,0:T(8,128)(2,1)S(1)}, bf16[512,768]{1,0:T(8,128)(2,1)S(1)}, u32[]{:S(2)}, u32[]{:S(2)}) collective-permute-start(bf16[512,768]{1,0:T(8,128)(2,1)S(1)} %add_convert_fusion.5), channel_id=1, source_target_pairs={{0,1},{1,0},{2,3},{3,2},{4,5},{5,4},{6,7},{7,6},{8,9},{9,8},{10,11... | collective-permute-start | bytes 2359304 | tf_op jit(solution)/shard_map/ppermute | solution.py:22
  589.4 84.7 %copy-start.41 = (bf16[1024,768]{1,0:T(8,128)(2,1)}, bf16[1024,768]{1,0:T(8,128)(2,1)S(1)}, u32[]{:S(2)}) copy-start(bf16[1024,768]{1,0:T(8,128)(2,1)S(1)} %maximum_select_fusion.3) | copy-start | bytes 4718596
  589.4 70.1 %collective-permute-start.3 = (bf16[1024,768]{1,0:T(8,128)(2,1)S(1)}, bf16[1024,768]{1,0:T(8,128)(2,1)S(1)}, u32[]{:S(2)}, u32[]{:S(2)}) collective-permute-start(bf16[1024,768]{1,0:T(8,128)(2,1)S(1)} %maximum_select_fusion.3), channel_id=1, source_target_pairs={{0,2},{1,3},{2,0},{3,1},{4,6},{5,7},{6,4},{7,5},{8,10},{9,11},{10,... | collective-permute-start | bytes 4718600 | tf_op jit(solution)/shard_map/ppermute | solution.py:22
  683.7 106.8 %reduce-scatter.17.cloned.1.call-start = ((), (), s32[]{:S(2)}) async-start(), calls=%async_computation.13 | async-start | bytes 1327104 | tf_op jit(solution)/shard_map/reduce_scatter | solution.py:248
  691.5 133.7 %reduce-scatter.15.cloned.1.call-start = ((), (), s32[]{:S(2)}) async-start(), calls=%async_computation.12 | async-start | bytes 1327104 | tf_op jit(solution)/shard_map/reduce_scatter | solution.py:248
  717.5 198.0 %all-reduce.14.cloned.1.call-start = ((), (), s32[]{:S(2)}) async-start(), calls=%async_computation.15 | async-start | bytes 9437184
  741.6 488.6 %all-reduce.12.cloned.1.call-start = ((), (), s32[]{:S(2)}) async-start(), calls=%async_computation.14 | async-start | bytes 37748736 | tf_op jit(solution)/shard_map/psum | solution.py:241
  787.7 176.1 %copy-start.20 = (f32[512,768]{1,0:T(8,128)S(1)}, f32[512,768]{1,0:T(8,128)}, u32[]{:S(2)}) copy-start(f32[512,768]{1,0:T(8,128)} %copy-done.18) | copy-start | bytes 4718596
  787.7 176.1 %copy-start.35 = (bf16[12,64,512]{2,1,0:T(8,128)(2,1)S(1)}, bf16[12,64,512]{2,1,0:T(8,128)(2,1)}, u32[]{:S(2)}) copy-start(bf16[12,64,512]{2,1,0:T(8,128)(2,1)} %copy-done.34) | copy-start | bytes 2359300
  787.8 176.1 %copy-start.45 = (bf16[12,64,512]{2,1,0:T(8,128)(2,1)S(1)}, bf16[12,64,512]{2,1,0:T(8,128)(2,1)}, u32[]{:S(2)}) copy-start(bf16[12,64,512]{2,1,0:T(8,128)(2,1)} %copy-done.44) | copy-start | bytes 2359300
  (82 other events, 520.1 us)
Sparse Core Ops, SparseCore 0:
  32.4 66.1 all-gather.2
  117.1 58.8 reduce-scatter.6
  201.7 63.5 all-gather.4
  283.8 58.8 reduce-scatter.8
  469.2 60.3 reduce-scatter.10
  683.8 60.3 reduce-scatter.12
  747.9 36.8 reduce-scatter.16
  788.4 36.7 reduce-scatter.14
  828.5 86.9 all-reduce.13
  923.5 306.5 all-reduce.11
